TPU v7x, 128 devices: a whole 4x4x4 slice. The times are simulated.
128 devices in a mesh: ctx: 64 (over z, x_hi, y, core), head: 2 (over x_lo).
Axes of the slice: x: 4 (x_hi: 2, x_lo: 2; x = x_hi * 2 + x_lo), y: 4, z: 4, core: 2. Of those that a mesh axis runs over, the one named last changes fastest.
Arguments:
- queries: bfloat16 [64, 1024, 2048], P('ctx', None, 'head'), may hold values from -8 to 8
- keys: bfloat16 [64, 1024, 2048], P('ctx', None, 'head'), may hold values from -8 to 8
- values: bfloat16 [64, 1024, 2048], P('ctx', None, 'head'), may hold values from -24 to 24
- w_out: bfloat16 [2048, 4096], P('head'), may hold values from -0.125 to 0.125
Outputs:
- mixed: bfloat16 [64, 1024, 4096], P('ctx', 'head')
All inputs are finite; a program needn't handle non-finite values.
Results may differ from a plain program's by a relative error of at most 0.013.
Values may be sent and summed in bfloat16 or wider, within the bound.
No kernel may reach another device: no remote copies, remote signals or barrier semaphores. Data moves between devices by JAX's collectives and lax.ppermute only.
A program may use at most 128 MiB of HBM per device.

v0:
```python
import jax
import jax.numpy as jnp
from jax import lax
from jax.sharding import PartitionSpec as P

HD = 128
GROUP = 4
masked_score = -1e30


def in_blocks(x, dim, devices):
    before, after = (x.shape[:dim], x.shape[dim + 1 :])
    return jnp.moveaxis(x.reshape(*before, devices, -1, *after), dim, 0)


def summed_on_arrival(x, axis, dim):
    devices = lax.axis_size(axis)
    parts = lax.all_to_all(in_blocks(x, dim, devices), axis, 0, 0, tiled=True)
    return jnp.sum(parts.astype(jnp.float32), axis=0)


def split_kinds(tensor, parity):
    groups = tensor.shape[2] // (2 * GROUP * HD)
    shaped = tensor.reshape((tensor.shape[0], tensor.shape[1], groups, 2, GROUP, HD))
    return shaped[:, :, :, parity].reshape((tensor.shape[0], tensor.shape[1], groups * GROUP, HD))


def normalized(scores):
    top = jnp.max(scores, axis=-1, keepdims=True)
    expo = jnp.exp(scores - top)
    total = jnp.sum(expo, axis=-1, keepdims=True)
    return (expo / total).astype(jnp.bfloat16)


def row_attention(queries, keys, values):
    scale = jnp.float32(1.0 / HD**0.5)
    length = queries.shape[1]
    causal = lax.broadcasted_iota(jnp.int32, (length, length), 1) <= lax.broadcasted_iota(
        jnp.int32, (length, length), 0
    )

    def one_row(triple):
        query_row, key_row, value_row = triple
        scores = (
            jnp.einsum("qhd,khd->hqk", query_row, key_row, preferred_element_type=jnp.float32)
            * scale
        )
        scores = jnp.where(causal, scores, masked_score)
        weights = normalized(scores)
        return jnp.einsum(
            "hqk,khd->qhd", weights, value_row, preferred_element_type=jnp.float32
        ).astype(jnp.bfloat16)

    return lax.map(one_row, (queries, keys, values))


def column_attention(triple):
    queries, keys, values = triple
    scale = jnp.float32(1.0 / HD**0.5)
    height = queries.shape[0]
    causal = lax.broadcasted_iota(jnp.int32, (height, height), 1) <= lax.broadcasted_iota(
        jnp.int32, (height, height), 0
    )
    scores = (
        jnp.einsum("rchd,schd->chrs", queries, keys, preferred_element_type=jnp.float32) * scale
    )
    scores = jnp.where(causal, scores, masked_score)
    weights = normalized(scores)
    attended = jnp.einsum(
        "chrs,schd->rchd", weights, values, preferred_element_type=jnp.float32
    ).astype(jnp.bfloat16)
    return lax.all_to_all(attended, "ctx", split_axis=0, concat_axis=1, tiled=True)


def on_device(queries, keys, values, w_out):
    rows_dev, stride, local_feat = queries.shape
    model_width = w_out.shape[1]
    groups = local_feat // (2 * GROUP * HD)
    row_out = row_attention(split_kinds(queries, 0), split_kinds(keys, 0), split_kinds(values, 0))
    col_triple = (split_kinds(queries, 1), split_kinds(keys, 1), split_kinds(values, 1))
    col_out = column_attention(
        (
            lax.all_to_all(col_triple[0], "ctx", split_axis=1, concat_axis=0, tiled=True),
            lax.all_to_all(col_triple[1], "ctx", split_axis=1, concat_axis=0, tiled=True),
            lax.all_to_all(col_triple[2], "ctx", split_axis=1, concat_axis=0, tiled=True),
        )
    )
    joined = jnp.stack(
        [
            row_out.reshape((rows_dev, stride, groups, GROUP, HD)),
            col_out.reshape((rows_dev, stride, groups, GROUP, HD)),
        ],
        axis=3,
    ).reshape((rows_dev * stride, local_feat))
    partial_value = jnp.dot(joined, w_out, preferred_element_type=jnp.float32)
    partial_value = partial_value.reshape((rows_dev, stride, model_width))
    return summed_on_arrival(partial_value.astype(jnp.bfloat16), "head", 1).astype(jnp.bfloat16)


def solution(mesh):
    return jax.shard_map(
        on_device,
        mesh=mesh,
        in_specs=(
            P("ctx", None, "head"),
            P("ctx", None, "head"),
            P("ctx", None, "head"),
            P("head", None),
        ),
        out_specs=P("ctx", "head", None),
        check_vma=False,
    )
```

profile of v0, /device:TPU:1, one launch (start us, length us, event | category | flops | bytes accessed | tf_op | source)
XLA Modules:
  0.0 234.4 jit_solution(8424355942385947717)
XLA Ops:
  0.0 2.9 %copy.40 = bf16[1,1024,1024]{1,2,0:T(8,128)(2,1)S(1)} copy(bf16[1,1024,1024]{2,1,0:T(8,128)(2,1)} %param.5) | data formatting | bytes 4194304 | tf_op args[1]
  2.9 0.0 copy-start
  2.9 0.1 slice_bitcast_fusion.1
  3.0 1.7 copy.46
  4.7 0.0 copy-done
  4.7 12.7 %all-to-all-start.1 = ((bf16[1,1024,4,128]{3,2,0,1:T(4,128)(2,1)}), bf16[1,1024,4,128]{3,2,0,1:T(4,128)(2,1)}, u32[]{:S(2)}, u32[]{:S(2)}) async-start(bf16[1,1024,4,128]{3,2,0,1:T(4,128)(2,1)} %copy.46), calls=%async_computation.1 | async-start | bytes 2097152 | tf_op jit(solution)/shard_map/all_to_all | solution.py:84
  17.3 2.9 %copy.38 = bf16[1,1024,1024]{1,2,0:T(8,128)(2,1)S(1)} copy(bf16[1,1024,1024]{2,1,0:T(8,128)(2,1)} %param.4) | data formatting | bytes 4194304 | tf_op args[0]
  20.2 0.0 copy-start.1
  20.2 0.1 slice_bitcast_fusion.2
  20.3 1.6 copy.44
  21.9 0.0 copy-done.1
  21.9 14.8 %all-to-all-done.1 = bf16[1,1024,4,128]{3,2,0,1:T(4,128)(2,1)} async-done(((bf16[1,1024,4,128]{3,2,0,1:T(4,128)(2,1)}), bf16[1,1024,4,128]{3,2,0,1:T(4,128)(2,1)}, u32[]{:S(2)}, u32[]{:S(2)}) %all-to-all-start.1) | async-done | bytes 1048608 | tf_op jit(solution)/shard_map/all_to_all | solution.py:84
  36.7 5.2 %all-to-all-start = ((bf16[1,1024,4,128]{3,2,0,1:T(4,128)(2,1)}), bf16[1,1024,4,128]{3,2,0,1:T(4,128)(2,1)}, u32[]{:S(2)}, u32[]{:S(2)}) async-start(bf16[1,1024,4,128]{3,2,0,1:T(4,128)(2,1)} %copy.44), calls=%async_computation | async-start | bytes 2097152 | tf_op jit(solution)/shard_map/all_to_all | solution.py:83
  41.9 2.9 %copy.42 = bf16[1,1024,1024]{1,2,0:T(8,128)(2,1)S(1)} copy(bf16[1,1024,1024]{2,1,0:T(8,128)(2,1)} %param.6) | data formatting | bytes 4194304 | tf_op args[2]
  44.7 0.1 slice_bitcast_fusion
  44.8 1.5 copy.50
  46.3 1.3 iota_compare_fusion
  47.6 13.7 %all-to-all-done = bf16[1,1024,4,128]{3,2,0,1:T(4,128)(2,1)} async-done(((bf16[1,1024,4,128]{3,2,0,1:T(4,128)(2,1)}), bf16[1,1024,4,128]{3,2,0,1:T(4,128)(2,1)}, u32[]{:S(2)}, u32[]{:S(2)}) %all-to-all-start) | async-done | bytes 1048608 | tf_op jit(solution)/shard_map/all_to_all | solution.py:83
  61.4 4.7 %all-to-all-start.2 = ((bf16[1,1024,4,128]{3,2,0,1:T(4,128)(2,1)}), bf16[1,1024,4,128]{3,2,0,1:T(4,128)(2,1)S(1)}, u32[]{:S(2)}, u32[]{:S(2)}) async-start(bf16[1,1024,4,128]{3,2,0,1:T(4,128)(2,1)} %copy.50), calls=%async_computation.2 | async-start | bytes 2097152 | tf_op jit(solution)/shard_map/all_to_all | solution.py:85
  66.0 11.7 %fusion.43 = (f32[4,1024]{1,0:T(4,128)S(1)}, f32[4,1024,1024]{1,2,0:T(8,128)}) fusion(pred[1024,1024]{0,1:T(8,128)(4,1)} %iota_compare_fusion, bf16[1,1024,1,2,4,128]{1,5,4,3,2,0:T(8,128)(2,1)} %bitcast.59, bf16[1,1024,1,2,4,128]{1,5,4,3,2,0:T(8,128)(2,1)} %bitcast.57), kind=kOutput, calls=%fused_computation.43 | convolution fusion | flops 1090520064 | bytes 19939328 | tf_op jit(solution)/shard_map/while/body/eval_jaxpr/sub | solution.py:30
  77.8 4.8 %fusion.38 = (f32[16,4,64]{2,1,0:T(4,128)S(1)}, f32[16,4,64,64]{2,3,1,0:T(8,128)}) fusion(pred[64,64]{0,1:T(8,128)(4,1)S(1)} %iota_compare_fusion.1, bf16[64,16,4,128]{3,2,1,0:T(4,128)(2,1)} %bitcast.11, bf16[64,16,4,128]{3,2,1,0:T(4,128)(2,1)} %bitcast.9), kind=kOutput, calls=%fused_computation.42 | convolution fusion | flops 68157504 | bytes 3166208 | tf_op jit(solution)/shard_map/sub | solution.py:30
  82.6 2.9 %all-to-all-done.2 = bf16[1,1024,4,128]{3,2,0,1:T(4,128)(2,1)S(1)} async-done(((bf16[1,1024,4,128]{3,2,0,1:T(4,128)(2,1)}), bf16[1,1024,4,128]{3,2,0,1:T(4,128)(2,1)S(1)}, u32[]{:S(2)}, u32[]{:S(2)}) %all-to-all-start.2) | async-done | bytes 1048608 | tf_op jit(solution)/shard_map/all_to_all | solution.py:85
  85.5 2.9 %fusion.11 = bf16[64,16,4,128]{3,0,2,1:T(8,128)(2,1)S(1)} fusion(f32[16,4,64,64]{2,3,1,0:T(8,128)} %get-tuple-element.16, bf16[64,16,4,128]{3,2,1,0:T(4,128)(2,1)S(1)} %bitcast.62, f32[16,4,64]{2,1,0:T(4,128)S(1)} %get-tuple-element.15), kind=kOutput, calls=%fused_computation.20 | convolution fusion | flops 68157440 | bytes 3162112 | tf_op jit(solution)/shard_map/chrs,schd->rchd/dot_general | solution.py:69
  88.4 1.8 copy.54
  90.2 7.4 %all-to-all-start.3 = ((bf16[64,16,4,128]{3,2,1,0:T(4,128)(2,1)}), bf16[64,16,4,128]{3,2,1,0:T(4,128)(2,1)S(1)}, u32[]{:S(2)}, u32[]{:S(2)}) async-start(bf16[64,16,4,128]{3,2,1,0:T(4,128)(2,1)} %copy.54), calls=%async_computation.3 | async-start | bytes 2097152 | tf_op jit(solution)/shard_map/all_to_all | solution.py:72
  97.6 8.1 %fusion.12 = bf16[1,1024,1,1,4,128]{1,5,4,3,2,0:T(8,128)(2,1)} fusion(f32[4,1024,1024]{1,2,0:T(8,128)} %get-tuple-element.24, f32[4,1024]{1,0:T(4,128)S(1)} %get-tuple-element.17, bf16[1,1024,1,2,4,128]{1,5,4,3,2,0:T(8,128)(2,1)S(1)} %bitcast.55), kind=kOutput, calls=%fused_computation.21 | convolution fusion | flops 1082654720 | bytes 18890752 | tf_op jit(solution)/shard_map/while/body/eval_jaxpr/hqk,khd->qhd/dot_general | solution.py:50
  105.7 11.4 %all-to-all-done.3 = bf16[64,16,4,128]{3,2,1,0:T(4,128)(2,1)S(1)} async-done(((bf16[64,16,4,128]{3,2,1,0:T(4,128)(2,1)}), bf16[64,16,4,128]{3,2,1,0:T(4,128)(2,1)S(1)}, u32[]{:S(2)}, u32[]{:S(2)}) %all-to-all-start.3) | async-done | bytes 1048608 | tf_op jit(solution)/shard_map/all_to_all | solution.py:72
  117.1 0.7 copy.56
  117.7 0.2 pad_maximum_fusion
  117.9 11.4 %convolution_convert_fusion = bf16[1024,4096]{1,0:T(8,128)(2,1)S(1)} fusion(bf16[1024,1024]{0,1:T(8,128)(2,1)S(1)} %bitcast.61, bf16[1024,4096]{1,0:T(8,128)(2,1)} %param.7), kind=kOutput, calls=%fused_computation.10 | convolution fusion | flops 8594128896 | bytes 18874368 | tf_op jit(solution)/shard_map/dot_general | solution.py:95
  129.3 96.4 %all_to_all.50 = bf16[2,1,512,4096]{3,2,1,0:T(8,128)(2,1)} all-to-all(bf16[2,1,512,4096]{3,2,1,0:T(8,128)(2,1)S(1)} %bitcast.53), channel_id=1, replica_groups=mesh['ctx'=64,'head'=2] {'head'}, dimensions={0} | all-to-all | bytes 16777216 | tf_op jit(solution)/shard_map/all_to_all | solution.py:18
  225.7 8.6 %reduce_sum.35 = bf16[512,4096]{1,0:T(8,128)(2,1)} reduce(bf16[2,1,512,4096]{3,2,1,0:T(8,128)(2,1)} %all_to_all.50, bf16[]{:T(256)} %constant.29.clone.1), dimensions={0,1}, to_apply=%region_4.5 | reduce | flops 2097152 | bytes 12582914 | tf_op jit(solution)/shard_map/reduce_sum | solution.py:19
  (3 shorter events, 0.0 us)
Async XLA Ops:
  2.9 1.8 copy-start
  4.7 32.0 %all-to-all-start.1 = ((bf16[1,1024,4,128]{3,2,0,1:T(4,128)(2,1)}), bf16[1,1024,4,128]{3,2,0,1:T(4,128)(2,1)}, u32[]{:S(2)}, u32[]{:S(2)}) async-start(bf16[1,1024,4,128]{3,2,0,1:T(4,128)(2,1)} %copy.46), calls=%async_computation.1 | async-start | bytes 2097152 | tf_op jit(solution)/shard_map/all_to_all | solution.py:84
  20.2 1.7 copy-start.1
  36.7 24.7 %all-to-all-start = ((bf16[1,1024,4,128]{3,2,0,1:T(4,128)(2,1)}), bf16[1,1024,4,128]{3,2,0,1:T(4,128)(2,1)}, u32[]{:S(2)}, u32[]{:S(2)}) async-start(bf16[1,1024,4,128]{3,2,0,1:T(4,128)(2,1)} %copy.44), calls=%async_computation | async-start | bytes 2097152 | tf_op jit(solution)/shard_map/all_to_all | solution.py:83
  61.4 24.1 %all-to-all-start.2 = ((bf16[1,1024,4,128]{3,2,0,1:T(4,128)(2,1)}), bf16[1,1024,4,128]{3,2,0,1:T(4,128)(2,1)S(1)}, u32[]{:S(2)}, u32[]{:S(2)}) async-start(bf16[1,1024,4,128]{3,2,0,1:T(4,128)(2,1)} %copy.50), calls=%async_computation.2 | async-start | bytes 2097152 | tf_op jit(solution)/shard_map/all_to_all | solution.py:85
  90.2 26.9 %all-to-all-start.3 = ((bf16[64,16,4,128]{3,2,1,0:T(4,128)(2,1)}), bf16[64,16,4,128]{3,2,1,0:T(4,128)(2,1)S(1)}, u32[]{:S(2)}, u32[]{:S(2)}) async-start(bf16[64,16,4,128]{3,2,1,0:T(4,128)(2,1)} %copy.54), calls=%async_computation.3 | async-start | bytes 2097152 | tf_op jit(solution)/shard_map/all_to_all | solution.py:72
  105.7 12.1 %copy-start.2 = (bf16[1,1024,1,1,4,128]{1,5,4,3,2,0:T(8,128)(2,1)S(1)}, bf16[1,1024,1,1,4,128]{1,5,4,3,2,0:T(8,128)(2,1)}, u32[]{:S(2)}) copy-start(bf16[1,1024,1,1,4,128]{1,5,4,3,2,0:T(8,128)(2,1)} %fusion.12) | copy-start | bytes 3145732
where the time goes:
time: 235 us; the launch traced here: 234 us
  blocking collectives  96.4 us (41%)
  waiting for transfers between devices  42.8 us (18%)
  matrix products  38.9 us (17%)
  starting transfers between devices  30 us (13%)
  local copies, waits for them, and re-layouts  16 us (7%)
  other arithmetic  10.2 us (4%)
    all_to_all x1, blocking collectives, summed_on_arrival(): parts = lax.all_to_all(in_blocks(x, dim, devices), axis, 0, 0, tiled=True)  96.4 us
    sub x2, matrix products, normalized(): expo = jnp.exp(scores - top)  16.5 us
    all_to_all x1, waiting for transfers between devices, on_device(): lax.all_to_all(col_triple[1], 'ctx', split_axis=1, concat_axis=0, tiled=T...  14.8 us
    all_to_all x1, waiting for transfers between devices, on_device(): lax.all_to_all(col_triple[0], 'ctx', split_axis=1, concat_axis=0, tiled=T...  13.7 us
    all_to_all x1, starting transfers between devices, on_device(): lax.all_to_all(col_triple[1], 'ctx', split_axis=1, concat_axis=0, tiled=T...  12.7 us
    dot_general x1, matrix products, on_device(): partial_value = jnp.dot(joined, w_out, preferred_element_type=jnp.float32)  11.4 us
    all_to_all x1, waiting for transfers between devices, column_attention(): lax.all_to_all(attended, 'ctx', split_axis=0, concat_axis=1, tiled=True)  11.4 us
    reduce_sum x1, other arithmetic, summed_on_arrival(): return jnp.sum(parts.astype(jnp.float32), axis=0)  8.63 us
  transfers between devices with their start and end apart: 4, of which 4 were waited for; matrix products, arithmetic and copies ran while one was open for 15% of the time, Pallas kernels for 0%

commit v1 on v0

--- a/solution.py
+++ b/solution.py
@@ -1,3 +1,4 @@
+import functools
 import jax
 import jax.numpy as jnp
 from jax import lax
@@ -6,6 +7,22 @@
 HD = 128
 GROUP = 4
 masked_score = -1e30
+
+
+def _pair_inputs(my_tile, axis_no, d_out):
+    right_arr = jnp.concatenate(
+        lax.all_to_all(
+            jnp.stack(jnp.split(my_tile, lax.axis_size("ctx"), axis=axis_no)),
+            "ctx",
+            split_axis=0,
+            concat_axis=0,
+        ),
+        axis=d_out,
+    )
+    return right_arr
+
+
+shape_the_set = functools.partial(_pair_inputs, axis_no=0, d_out=1)
 
 
 def in_blocks(x, dim, devices):
@@ -69,7 +86,7 @@
     attended = jnp.einsum(
         "chrs,schd->rchd", weights, values, preferred_element_type=jnp.float32
     ).astype(jnp.bfloat16)
-    return lax.all_to_all(attended, "ctx", split_axis=0, concat_axis=1, tiled=True)
+    return shape_the_set(attended)
 
 
 def on_device(queries, keys, values, w_out):

time: 235 us -> 275 us (1.17)
  local copies, waits for them, and re-layouts: 16 us -> 55.6 us
    unnamed x9 -> x72, local copies, waits for them, and re-layouts: 8.59 us -> 47.1 us
    all_to_all x1, starting transfers between devices: 5.19 us -> 12.7 us  [on_device(): lax.all_to_all(col_triple[0], 'ctx', split_axis=1, concat_axis=0, tiled=T...]
    all_to_all x1, starting transfers between devices: 12.7 us -> 5.19 us  [on_device(): lax.all_to_all(col_triple[1], 'ctx', split_axis=1, concat_axis=0, tiled=T...]
  transfers between devices with their start and end apart: 4 -> 4, of which waited for: 4 -> 4; matrix products, arithmetic and copies ran while one was open for 15% -> 13% of each run, Pallas kernels for 0% -> 0%
where the time goes in v1:
time: 275 us; the launch traced here: 274 us
  blocking collectives  96.4 us (35%)
  local copies, waits for them, and re-layouts  55.6 us (20%)
  waiting for transfers between devices  42.8 us (16%)
  matrix products  38.9 us (14%)
  starting transfers between devices  30 us (11%)
  other arithmetic  10.2 us (4%)
    all_to_all x1, blocking collectives, summed_on_arrival(): parts = lax.all_to_all(in_blocks(x, dim, devices), axis, 0, 0, tiled=True)  96.4 us
    unnamed x72, local copies, waits for them, and re-layouts  47.1 us
    sub x2, matrix products, normalized(): expo = jnp.exp(scores - top)  16.6 us
    all_to_all x1, waiting for transfers between devices, on_device(): lax.all_to_all(col_triple[0], 'ctx', split_axis=1, concat_axis=0, tiled=T...  14.8 us
    all_to_all x1, waiting for transfers between devices, on_device(): lax.all_to_all(col_triple[1], 'ctx', split_axis=1, concat_axis=0, tiled=T...  13.7 us
    all_to_all x1, starting transfers between devices, on_device(): lax.all_to_all(col_triple[0], 'ctx', split_axis=1, concat_axis=0, tiled=T...  12.7 us
    dot_general x1, matrix products, on_device(): partial_value = jnp.dot(joined, w_out, preferred_element_type=jnp.float32)  11.4 us
    all_to_all x1, waiting for transfers between devices, _pair_inputs(): lax.all_to_all(jnp.stack(jnp.split(my_tile, lax.axis_size('ctx'), axis=ax...  11.4 us
  transfers between devices with their start and end apart: 4, of which 4 were waited for; matrix products, arithmetic and copies ran while one was open for 13% of the time, Pallas kernels for 0%

profile of v1, /device:TPU:1, one launch (start us, length us, event | category | flops | bytes accessed | tf_op | source)
XLA Modules:
  0.0 274.2 jit_solution(10978007434938377049)
XLA Ops:
  0.0 2.9 %copy.2953 = bf16[1,1024,1024]{1,2,0:T(8,128)(2,1)S(1)} copy(bf16[1,1024,1024]{2,1,0:T(8,128)(2,1)} %param.4) | data formatting | bytes 4194304 | tf_op args[0]
  3.0 1.6 copy.2959
  4.6 12.7 %all-to-all-start = ((bf16[1,1024,4,128]{3,2,0,1:T(4,128)(2,1)}), bf16[1,1024,4,128]{3,2,0,1:T(4,128)(2,1)}, u32[]{:S(2)}, u32[]{:S(2)}) async-start(bf16[1,1024,4,128]{3,2,0,1:T(4,128)(2,1)} %copy.2959), calls=%async_computation | async-start | bytes 2097152 | tf_op jit(solution)/shard_map/all_to_all | solution.py:100
  17.2 2.9 %copy.2955 = bf16[1,1024,1024]{1,2,0:T(8,128)(2,1)S(1)} copy(bf16[1,1024,1024]{2,1,0:T(8,128)(2,1)} %param.5) | data formatting | bytes 4194304 | tf_op args[1]
  20.2 1.6 copy.2961
  21.8 14.8 %all-to-all-done = bf16[1,1024,4,128]{3,2,0,1:T(4,128)(2,1)} async-done(((bf16[1,1024,4,128]{3,2,0,1:T(4,128)(2,1)}), bf16[1,1024,4,128]{3,2,0,1:T(4,128)(2,1)}, u32[]{:S(2)}, u32[]{:S(2)}) %all-to-all-start) | async-done | bytes 1048608 | tf_op jit(solution)/shard_map/all_to_all | solution.py:100
  36.6 5.2 %all-to-all-start.1 = ((bf16[1,1024,4,128]{3,2,0,1:T(4,128)(2,1)}), bf16[1,1024,4,128]{3,2,0,1:T(4,128)(2,1)}, u32[]{:S(2)}, u32[]{:S(2)}) async-start(bf16[1,1024,4,128]{3,2,0,1:T(4,128)(2,1)} %copy.2961), calls=%async_computation.1 | async-start | bytes 2097152 | tf_op jit(solution)/shard_map/all_to_all | solution.py:101
  41.8 2.9 %copy.2957 = bf16[1,1024,1024]{1,2,0:T(8,128)(2,1)S(1)} copy(bf16[1,1024,1024]{2,1,0:T(8,128)(2,1)} %param.6) | data formatting | bytes 4194304 | tf_op args[2]
  44.7 1.5 copy.2965
  46.2 1.3 iota_compare_fusion
  47.5 13.7 %all-to-all-done.1 = bf16[1,1024,4,128]{3,2,0,1:T(4,128)(2,1)} async-done(((bf16[1,1024,4,128]{3,2,0,1:T(4,128)(2,1)}), bf16[1,1024,4,128]{3,2,0,1:T(4,128)(2,1)}, u32[]{:S(2)}, u32[]{:S(2)}) %all-to-all-start.1) | async-done | bytes 1048608 | tf_op jit(solution)/shard_map/all_to_all | solution.py:101
  61.3 4.7 %all-to-all-start.2 = ((bf16[1,1024,4,128]{3,2,0,1:T(4,128)(2,1)}), bf16[1,1024,4,128]{3,2,0,1:T(4,128)(2,1)S(1)}, u32[]{:S(2)}, u32[]{:S(2)}) async-start(bf16[1,1024,4,128]{3,2,0,1:T(4,128)(2,1)} %copy.2965), calls=%async_computation.2 | async-start | bytes 2097152 | tf_op jit(solution)/shard_map/all_to_all | solution.py:102
  66.0 11.8 %fusion.47 = (f32[4,1024]{1,0:T(4,128)S(1)}, f32[4,1024,1024]{1,2,0:T(8,128)}) fusion(pred[1024,1024]{0,1:T(8,128)(4,1)} %iota_compare_fusion, bf16[1,1024,1,2,4,128]{1,5,4,3,2,0:T(8,128)(2,1)} %bitcast.186, bf16[1,1024,1,2,4,128]{1,5,4,3,2,0:T(8,128)(2,1)} %bitcast.188), kind=kOutput, calls=%fused_computation.142 | convolution fusion | flops 1090520064 | bytes 19939328 | tf_op jit(solution)/shard_map/while/body/eval_jaxpr/sub | solution.py:47
  77.7 4.8 %fusion.42 = (f32[16,4,64]{2,1,0:T(4,128)S(1)}, f32[16,4,64,64]{2,3,1,0:T(8,128)}) fusion(pred[64,64]{0,1:T(8,128)(4,1)S(1)} %iota_compare_fusion.1, bf16[64,16,4,128]{3,2,1,0:T(4,128)(2,1)} %bitcast.11, bf16[64,16,4,128]{3,2,1,0:T(4,128)(2,1)} %bitcast.9), kind=kOutput, calls=%fused_computation.141 | convolution fusion | flops 68157504 | bytes 3166208 | tf_op jit(solution)/shard_map/sub | solution.py:47
  82.5 2.9 %all-to-all-done.2 = bf16[1,1024,4,128]{3,2,0,1:T(4,128)(2,1)S(1)} async-done(((bf16[1,1024,4,128]{3,2,0,1:T(4,128)(2,1)}), bf16[1,1024,4,128]{3,2,0,1:T(4,128)(2,1)S(1)}, u32[]{:S(2)}, u32[]{:S(2)}) %all-to-all-start.2) | async-done | bytes 1048608 | tf_op jit(solution)/shard_map/all_to_all | solution.py:102
  85.4 2.9 %fusion.11 = bf16[64,16,4,128]{3,0,2,1:T(8,128)(2,1)S(1)} fusion(f32[16,4,64,64]{2,3,1,0:T(8,128)} %get-tuple-element.88, bf16[64,16,4,128]{3,2,1,0:T(4,128)(2,1)S(1)} %bitcast.191, f32[16,4,64]{2,1,0:T(4,128)S(1)} %get-tuple-element.87), kind=kOutput, calls=%fused_computation.20 | convolution fusion | flops 68157440 | bytes 3162112 | tf_op jit(solution)/shard_map/chrs,schd->rchd/dot_general | solution.py:86
  88.5 0.7 fusion.40
  89.1 0.7 fusion.38
  89.8 0.7 fusion.39
  90.5 0.6 constant_dynamic-update-slice_fusion.63
  91.3 0.6 constant_dynamic-update-slice_fusion.62
  92.0 0.6 constant_dynamic-update-slice_fusion.61
  92.6 0.6 constant_dynamic-update-slice_fusion.60
  93.2 0.6 constant_dynamic-update-slice_fusion.59
  93.8 0.6 constant_dynamic-update-slice_fusion.58
  129.9 7.5 %all-to-all-start.3 = ((bf16[64,1,16,4,128]{4,3,2,1,0:T(4,128)(2,1)}), bf16[64,1,16,4,128]{4,3,2,1,0:T(4,128)(2,1)S(1)}, u32[]{:S(2)}, u32[]{:S(2)}) async-start(bf16[64,1,16,4,128]{4,3,2,1,0:T(4,128)(2,1)} %constant_dynamic-update-slice_fusion), calls=%async_computation.3 | async-start | bytes 2097152 | tf_op jit(solution)/shard_map/all_to_all | solution.py:14
  137.4 8.1 %fusion.12 = bf16[1,1024,1,1,4,128]{1,5,4,3,2,0:T(8,128)(2,1)} fusion(f32[4,1024,1024]{1,2,0:T(8,128)} %get-tuple-element.90, f32[4,1024]{1,0:T(4,128)S(1)} %get-tuple-element.89, bf16[1,1024,1,2,4,128]{1,5,4,3,2,0:T(8,128)(2,1)S(1)} %bitcast.184), kind=kOutput, calls=%fused_computation.21 | convolution fusion | flops 1082654720 | bytes 18890752 | tf_op jit(solution)/shard_map/while/body/eval_jaxpr/hqk,khd->qhd/dot_general | solution.py:67
  145.4 11.4 %all-to-all-done.3 = bf16[64,1,16,4,128]{4,3,2,1,0:T(4,128)(2,1)S(1)} async-done(((bf16[64,1,16,4,128]{4,3,2,1,0:T(4,128)(2,1)}), bf16[64,1,16,4,128]{4,3,2,1,0:T(4,128)(2,1)S(1)}, u32[]{:S(2)}, u32[]{:S(2)}) %all-to-all-start.3) | async-done | bytes 1048608 | tf_op jit(solution)/shard_map/all_to_all | solution.py:14
  156.8 0.7 copy.3032
  157.7 11.4 %convolution_convert_fusion = bf16[1024,4096]{1,0:T(8,128)(2,1)S(1)} fusion(bf16[1024,1024]{0,1:T(8,128)(2,1)S(1)} %bitcast.190, bf16[1024,4096]{1,0:T(8,128)(2,1)} %param.7), kind=kOutput, calls=%fused_computation.10 | convolution fusion | flops 8594128896 | bytes 18874368 | tf_op jit(solution)/shard_map/dot_general | solution.py:112
  169.1 96.4 %all_to_all.46 = bf16[2,1,512,4096]{3,2,1,0:T(8,128)(2,1)} all-to-all(bf16[2,1,512,4096]{3,2,1,0:T(8,128)(2,1)S(1)} %bitcast.182), channel_id=1, replica_groups=mesh['ctx'=64,'head'=2] {'head'}, dimensions={0} | all-to-all | bytes 16777216 | tf_op jit(solution)/shard_map/all_to_all | solution.py:35
  265.6 8.6 %reduce_sum.35 = bf16[512,4096]{1,0:T(8,128)(2,1)} reduce(bf16[2,1,512,4096]{3,2,1,0:T(8,128)(2,1)} %all_to_all.46, bf16[]{:T(256)} %constant.29.clone.1), dimensions={0,1}, to_apply=%region_4.5 | reduce | flops 2097152 | bytes 12582914 | tf_op jit(solution)/shard_map/reduce_sum | solution.py:36
  (86 shorter events, 36.2 us)
Async XLA Ops:
  2.9 1.7 copy-start
  4.6 32.0 %all-to-all-start = ((bf16[1,1024,4,128]{3,2,0,1:T(4,128)(2,1)}), bf16[1,1024,4,128]{3,2,0,1:T(4,128)(2,1)}, u32[]{:S(2)}, u32[]{:S(2)}) async-start(bf16[1,1024,4,128]{3,2,0,1:T(4,128)(2,1)} %copy.2959), calls=%async_computation | async-start | bytes 2097152 | tf_op jit(solution)/shard_map/all_to_all | solution.py:100
  20.1 1.7 copy-start.1
  36.6 24.7 %all-to-all-start.1 = ((bf16[1,1024,4,128]{3,2,0,1:T(4,128)(2,1)}), bf16[1,1024,4,128]{3,2,0,1:T(4,128)(2,1)}, u32[]{:S(2)}, u32[]{:S(2)}) async-start(bf16[1,1024,4,128]{3,2,0,1:T(4,128)(2,1)} %copy.2961), calls=%async_computation.1 | async-start | bytes 2097152 | tf_op jit(solution)/shard_map/all_to_all | solution.py:101
  61.3 24.1 %all-to-all-start.2 = ((bf16[1,1024,4,128]{3,2,0,1:T(4,128)(2,1)}), bf16[1,1024,4,128]{3,2,0,1:T(4,128)(2,1)S(1)}, u32[]{:S(2)}, u32[]{:S(2)}) async-start(bf16[1,1024,4,128]{3,2,0,1:T(4,128)(2,1)} %copy.2965), calls=%async_computation.2 | async-start | bytes 2097152 | tf_op jit(solution)/shard_map/all_to_all | solution.py:102
  129.9 26.9 %all-to-all-start.3 = ((bf16[64,1,16,4,128]{4,3,2,1,0:T(4,128)(2,1)}), bf16[64,1,16,4,128]{4,3,2,1,0:T(4,128)(2,1)S(1)}, u32[]{:S(2)}, u32[]{:S(2)}) async-start(bf16[64,1,16,4,128]{4,3,2,1,0:T(4,128)(2,1)} %constant_dynamic-update-slice_fusion), calls=%async_computation.3 | async-start | bytes 2097152 | tf_op jit(solution)/shard_map/all_to_all | solution.py:14
  145.4 12.1 %copy-start.2 = (bf16[1,1024,1,1,4,128]{1,5,4,3,2,0:T(8,128)(2,1)S(1)}, bf16[1,1024,1,1,4,128]{1,5,4,3,2,0:T(8,128)(2,1)}, u32[]{:S(2)}) copy-start(bf16[1,1024,1,1,4,128]{1,5,4,3,2,0:T(8,128)(2,1)} %fusion.12) | copy-start | bytes 3145732
